TPU v7x, 32 devices: a whole 2x2x4 slice. The times are simulated.
32 devices in a mesh: dp: 16 (over z, y, x), mp: 2 (over core).
Axes of the slice: x: 2, y: 2, z: 4, core: 2. Of those that a mesh axis runs over, the one named last changes fastest.
Arguments:
- tokens: bfloat16 [16384, 768], P(('dp', 'mp')), may hold values from -8 to 8
- segment_ids: int32 [16, 1024], P('dp'), may hold values from 0 to 16, never falling along the last dimension, each value on 1 to 512 neighbouring positions
- query_weight: bfloat16 [768, 768], P(None, 'mp'), may hold values from -0.21875 to 0.21875
- key_weight: bfloat16 [768, 768], P(None, 'mp'), may hold values from -0.21875 to 0.21875
- value_weight: bfloat16 [768, 768], P(None, 'mp'), may hold values from -0.21875 to 0.21875
- output_weight: bfloat16 [768, 768], P('mp'), may hold values from -0.875 to 0.875
- inner_weight: bfloat16 [768, 3072], P(None, 'mp'), may hold values from -0.21875 to 0.21875
- outer_weight: bfloat16 [3072, 768], P('mp'), may hold values from -0.109375 to 0.109375
- mixer_down: bfloat16 [768, 64], replicated, may hold values from -0.21875 to 0.21875
- mixer_down_bias: bfloat16 [64], replicated, may hold values from -3 to 3
- mixer_up: bfloat16 [64, 768], replicated, may hold values from -0.75 to 0.75
- mixer_up_bias: bfloat16 [768], replicated, may hold values from -3 to 3
- dense_down: bfloat16 [768, 64], replicated, may hold values from -0.21875 to 0.21875
- dense_down_bias: bfloat16 [64], replicated, may hold values from -3 to 3
- dense_up: bfloat16 [64, 768], replicated, may hold values from -0.75 to 0.75
- dense_up_bias: bfloat16 [768], replicated, may hold values from -3 to 3
- first_gain: bfloat16 [768], replicated, may hold values from 0.5 to 1.5
- first_shift: bfloat16 [768], replicated, may hold values from -3 to 3
- second_gain: bfloat16 [768], replicated, may hold values from 0.5 to 1.5
- second_shift: bfloat16 [768], replicated, may hold values from -3 to 3
- output_grad: bfloat16 [16384, 768], P(('dp', 'mp')), may hold values from -6 to 6
Outputs:
- activations: bfloat16 [16384, 768], P(('dp', 'mp'))
- input_grad: bfloat16 [16384, 768], P(('dp', 'mp'))
- mixer_down_grad: float32 [768, 64], replicated
- mixer_down_bias_grad: float32 [64], replicated
- mixer_up_grad: float32 [64, 768], replicated
- mixer_up_bias_grad: float32 [768], replicated
- dense_down_grad: float32 [768, 64], replicated
- dense_down_bias_grad: float32 [64], replicated
- dense_up_grad: float32 [64, 768], replicated
- dense_up_bias_grad: float32 [768], replicated
- first_gain_grad: float32 [768], replicated
- first_shift_grad: float32 [768], replicated
- second_gain_grad: float32 [768], replicated
- second_shift_grad: float32 [768], replicated
- norm_ratios: float32 [2], replicated
Inputs may be any that keep to these rules, and one draw needn't show every extreme that they name: `segment_ids`: each row numbers the items of one packed batch from 0, never falling.
All inputs are finite; a program needn't handle non-finite values.
Results may differ from a plain program's by a relative error of at most 0.019.
Values may be sent and summed in bfloat16 or wider, within the bound.
No kernel may reach another device: no remote copies, remote signals or barrier semaphores. Data moves between devices by JAX's collectives and lax.ppermute only.
A program may use at most 128 MiB of HBM per device.

v0:
```python
import jax
import jax.numpy as jnp
from jax import lax
from jax.sharding import PartitionSpec as P

HEAD_DIM = 64
EPS = 1e-12
block_limit = 512


def gelu_value(values):
    return jax.nn.gelu(values, approximate=False)


def gelu_slope(values):
    return (
        0.5 * (1.0 + jax.scipy.special.erf(values * 0.7071067811865476))
        + values * jnp.exp(-0.5 * values * values) * 0.3989422804014327
    )


def times_transpose(left, right):
    return lax.dot_general(
        left, right, (((1,), (1,)), ((), ())), preferred_element_type=jnp.float32
    )


def contract_rows(left, right):
    return lax.dot_general(
        left, right, (((0,), (0,)), ((), ())), preferred_element_type=jnp.float32
    )


def norm_forward(residual, gain, shift):
    mean = jnp.mean(residual, -1, keepdims=True)
    centred = residual - mean
    reciprocal = lax.rsqrt(jnp.mean(centred * centred, -1, keepdims=True) + EPS)
    normed = centred * reciprocal
    return (normed * gain + shift, normed, reciprocal)


def norm_backward(upstream, normed, reciprocal, gain):
    scaled = upstream * gain
    inflow = reciprocal * (
        scaled
        - jnp.mean(scaled, -1, keepdims=True)
        - normed * jnp.mean(scaled * normed, -1, keepdims=True)
    )
    return (inflow, jnp.sum(upstream * normed, 0), jnp.sum(upstream, 0))


def adapter_forward(inflow, down, down_bias, up, up_bias):
    inflow_low = inflow.astype(jnp.bfloat16)
    inner = jnp.dot(inflow_low, down, preferred_element_type=jnp.float32) + down_bias.astype(
        jnp.float32
    )
    active = gelu_value(inner).astype(jnp.bfloat16)
    outflow = jnp.dot(active, up, preferred_element_type=jnp.float32) + up_bias.astype(jnp.float32)
    return (outflow, (inflow_low, inner, active))


def adapter_backward(grad_out, kept, down, up):
    inflow_low, inner, active = kept
    grad_top = grad_out.astype(jnp.bfloat16)
    up_grad = contract_rows(active, grad_top)
    up_bias_grad = jnp.sum(grad_top.astype(jnp.float32), 0)
    grad_mid = (times_transpose(grad_top, up) * gelu_slope(inner)).astype(jnp.bfloat16)
    down_grad = contract_rows(inflow_low, grad_mid)
    down_bias_grad = jnp.sum(grad_mid.astype(jnp.float32), 0)
    inflow_grad = times_transpose(grad_mid, down)
    return (inflow_grad, (down_grad, down_bias_grad, up_grad, up_bias_grad))


def score_block(query_rows, query_seg, keys, key_seg, scale):
    scores = (
        jnp.einsum("qhd,khd->hqk", query_rows, keys, preferred_element_type=jnp.float32) * scale
    )
    same = query_seg[:, None] == key_seg[None, :]
    return jnp.where(same[None], scores, -1e30)


def attention_forward(queries, keys, values, seg_row, block, scale):
    count = queries.shape[0] // block

    def one_block(index):
        start = index * block
        rows = lax.dynamic_slice_in_dim(queries, start, block, 0)
        row_seg = lax.dynamic_slice_in_dim(seg_row, start, block, 0)
        scores = score_block(rows, row_seg, keys, seg_row, scale)
        peak = jnp.max(scores, -1, keepdims=True)
        exponent = jnp.exp(scores - peak)
        total = jnp.sum(exponent, -1, keepdims=True)
        shares = (exponent / total).astype(jnp.bfloat16)
        mixed = jnp.einsum("hqk,khd->qhd", shares, values, preferred_element_type=jnp.float32)
        return (mixed.astype(jnp.bfloat16), (peak + jnp.log(total))[..., 0])

    mixed, log_totals = lax.map(one_block, jnp.arange(count))
    return (mixed.reshape(queries.shape), log_totals)


def attention_backward(queries, keys, values, seg_row, log_totals, mixed_grad, block, scale):
    count = queries.shape[0] // block

    def one_block(carry, index):
        key_grad, value_grad = carry
        start = index * block
        rows = lax.dynamic_slice_in_dim(queries, start, block, 0)
        row_seg = lax.dynamic_slice_in_dim(seg_row, start, block, 0)
        grad_rows = lax.dynamic_slice_in_dim(mixed_grad, start, block, 0)
        scores = score_block(rows, row_seg, keys, seg_row, scale)
        shares = jnp.exp(scores - log_totals[index][..., None])
        value_grad = value_grad + jnp.einsum(
            "hqk,qhd->khd",
            shares.astype(jnp.bfloat16),
            grad_rows,
            preferred_element_type=jnp.float32,
        )
        share_grad = jnp.einsum(
            "qhd,khd->hqk", grad_rows, values, preferred_element_type=jnp.float32
        )
        score_grad = (
            shares * (share_grad - jnp.sum(shares * share_grad, -1, keepdims=True))
        ).astype(jnp.bfloat16)
        query_grad = (
            jnp.einsum("hqk,khd->qhd", score_grad, keys, preferred_element_type=jnp.float32) * scale
        ).astype(jnp.bfloat16)
        key_grad = (
            key_grad
            + jnp.einsum("hqk,qhd->khd", score_grad, rows, preferred_element_type=jnp.float32)
            * scale
        )
        return ((key_grad, value_grad), query_grad)

    zeros = jnp.zeros(keys.shape, jnp.float32)
    (key_grad, value_grad), query_grad = lax.scan(one_block, (zeros, zeros), jnp.arange(count))
    return (
        query_grad.reshape(queries.shape),
        key_grad.astype(jnp.bfloat16),
        value_grad.astype(jnp.bfloat16),
    )


def per_device(
    tokens,
    segment_ids,
    query_weight,
    key_weight,
    value_weight,
    output_weight,
    inner_weight,
    outer_weight,
    mixer_down,
    mixer_down_bias,
    mixer_up,
    mixer_up_bias,
    dense_down,
    dense_down_bias,
    dense_up,
    dense_up_bias,
    first_gain,
    first_shift,
    second_gain,
    second_shift,
    output_grad,
):
    shard_rows = tokens.shape[0]
    group_rows = shard_rows * lax.axis_size("mp")
    seg_row = segment_ids[0]
    block = min(block_limit, group_rows)
    scale = HEAD_DIM ** (-0.5)
    width = query_weight.shape[1]
    local_heads = width // HEAD_DIM
    head_shape = (group_rows, local_heads, HEAD_DIM)
    gain_one = first_gain.astype(jnp.float32)
    gain_two = second_gain.astype(jnp.float32)
    piece = lax.all_gather(tokens, "mp", axis=0, tiled=True)
    projected = jnp.concatenate(
        [
            jnp.dot(piece, query_weight, preferred_element_type=jnp.float32).astype(jnp.bfloat16),
            jnp.dot(piece, key_weight, preferred_element_type=jnp.float32).astype(jnp.bfloat16),
            jnp.dot(piece, value_weight, preferred_element_type=jnp.float32).astype(jnp.bfloat16),
        ],
        1,
    )
    queries = projected[:, :width].reshape(head_shape)
    keys = projected[:, width : 2 * width].reshape(head_shape)
    values = projected[:, 2 * width :].reshape(head_shape)
    mixed, log_totals = attention_forward(queries, keys, values, seg_row, block, scale)
    mixed_flat = mixed.reshape(group_rows, width)
    attended = lax.psum_scatter(
        jnp.dot(mixed_flat, output_weight, preferred_element_type=jnp.float32),
        "mp",
        scatter_dimension=0,
        tiled=True,
    )
    token_values = tokens.astype(jnp.float32)
    mixer_out, mixer_kept = adapter_forward(
        attended, mixer_down, mixer_down_bias, mixer_up, mixer_up_bias
    )
    hidden, normed_one, recip_one = norm_forward(
        token_values + attended + mixer_out, gain_one, first_shift.astype(jnp.float32)
    )
    hidden_low = hidden.astype(jnp.bfloat16)
    inner = jnp.dot(
        lax.all_gather(hidden_low, "mp", axis=0, tiled=True),
        inner_weight,
        preferred_element_type=jnp.float32,
    )
    inner_low = gelu_value(inner).astype(jnp.bfloat16)
    dense_in = lax.psum_scatter(
        jnp.dot(inner_low, outer_weight, preferred_element_type=jnp.float32).astype(jnp.bfloat16),
        "mp",
        scatter_dimension=0,
        tiled=True,
    ).astype(jnp.float32)
    dense_out, dense_kept = adapter_forward(
        dense_in, dense_down, dense_down_bias, dense_up, dense_up_bias
    )
    result, normed_two, recip_two = norm_forward(
        hidden + dense_in + dense_out, gain_two, second_shift.astype(jnp.float32)
    )
    mixer_square = jnp.sum(mixer_out * mixer_out)
    dense_square = jnp.sum(dense_out * dense_out)
    input_square = jnp.sum(token_values * token_values)
    mixer_square, dense_square, input_square = lax.psum(
        (mixer_square, dense_square, input_square), ("dp", "mp")
    )
    upstream = output_grad.astype(jnp.float32)
    second_grad, second_gain_grad, second_shift_grad = norm_backward(
        upstream, normed_two, recip_two, gain_two
    )
    dense_back, dense_grads = adapter_backward(second_grad, dense_kept, dense_down, dense_up)
    dense_in_grad = (second_grad + dense_back).astype(jnp.bfloat16)
    inner_full = times_transpose(
        lax.all_gather(dense_in_grad, "mp", axis=0, tiled=True), outer_weight
    )
    inner_grad = (inner_full * gelu_slope(inner)).astype(jnp.bfloat16)
    hidden_back = lax.psum_scatter(
        times_transpose(inner_grad, inner_weight).astype(jnp.bfloat16),
        "mp",
        scatter_dimension=0,
        tiled=True,
    ).astype(jnp.float32)
    hidden_grad = second_grad + hidden_back
    first_grad, first_gain_grad, first_shift_grad = norm_backward(
        hidden_grad, normed_one, recip_one, gain_one
    )
    mixer_back, mixer_grads = adapter_backward(first_grad, mixer_kept, mixer_down, mixer_up)
    attended_grad = (first_grad + mixer_back).astype(jnp.bfloat16)
    mixed_grad = (
        times_transpose(lax.all_gather(attended_grad, "mp", axis=0, tiled=True), output_weight)
        .astype(jnp.bfloat16)
        .reshape(head_shape)
    )
    query_grad, key_grad, value_grad = attention_backward(
        queries, keys, values, seg_row, log_totals, mixed_grad, block, scale
    )
    query_flat = query_grad.reshape(group_rows, width)
    key_flat = key_grad.reshape(group_rows, width)
    value_flat = value_grad.reshape(group_rows, width)
    total = times_transpose(query_flat, query_weight)
    total = total + times_transpose(key_flat, key_weight)
    input_back = lax.psum_scatter(
        (total + times_transpose(value_flat, value_weight)).astype(jnp.bfloat16),
        "mp",
        scatter_dimension=0,
        tiled=True,
    ).astype(jnp.float32)
    input_grad = (first_grad + input_back).astype(jnp.bfloat16)
    summed = lax.psum(
        (
            mixer_grads[0],
            mixer_grads[1],
            mixer_grads[2],
            mixer_grads[3],
            dense_grads[0],
            dense_grads[1],
            dense_grads[2],
            dense_grads[3],
            first_gain_grad,
            first_shift_grad,
            second_gain_grad,
            second_shift_grad,
        ),
        ("dp", "mp"),
    )
    ratios = jnp.sqrt(jnp.stack([mixer_square, dense_square]) / input_square)
    return (
        result.astype(jnp.bfloat16),
        input_grad,
        summed[0],
        summed[1],
        summed[2],
        summed[3],
        summed[4],
        summed[5],
        summed[6],
        summed[7],
        summed[8],
        summed[9],
        summed[10],
        summed[11],
        ratios,
    )


def solution(mesh):
    placed = (
        P(("dp", "mp"), None),
        P("dp", None),
        P(None, "mp"),
        P(None, "mp"),
        P(None, "mp"),
        P("mp", None),
        P(None, "mp"),
        P("mp", None),
        P(),
        P(),
        P(),
        P(),
        P(),
        P(),
        P(),
        P(),
        P(),
        P(),
        P(),
        P(),
        P(("dp", "mp"), None),
    )
    return jax.shard_map(
        per_device,
        mesh=mesh,
        in_specs=placed,
        out_specs=(
            P(("dp", "mp"), None),
            P(("dp", "mp"), None),
            P(),
            P(),
            P(),
            P(),
            P(),
            P(),
            P(),
            P(),
            P(),
            P(),
            P(),
            P(),
            P(),
        ),
        check_vma=False,
    )
```

profile of v0, /device:TPU:0, one launch (start us, length us, event | category | flops | bytes accessed | tf_op | source)
XLA Modules:
  0.0 461.6 jit_solution(3610006697994505217)
XLA Ops:
  8.0 14.1 %all-gather.5.cloned.1.call-done = bf16[1024,768]{1,0:T(8,128)(2,1)} async-done(((bf16[512,768]{1,0:T(8,128)(2,1)}), bf16[1024,768]{1,0:T(8,128)(2,1)}) %all-gather.5.cloned.1.call-update) | async-done | bytes 1572880 | tf_op jit(solution)/shard_map/all_gather | solution.py:176
  29.1 27.5 %while.27 = (s32[]{:T(128)}, bf16[2,512,6,64]{1,3,2,0:T(8,128)(2,1)}, f32[2,6,512]{2,1,0:T(8,128)S(1)}, s32[2]{0:T(128)S(1)}, s32[1024]{0:T(1024)S(1)}, /*index=...) while((s32[]{:T(128)}, ...), condition=%wide.region_3.4_spmd, body=%wide.region_0.3_spmd.sunk | while | flops 843772928 | bytes 45472476 | solution.py:97
  37.8 5.0 %fusion.214 = bf16[2,512,6,64]{1,3,2,0:T(8,128)(2,1)} fusion(bf16[2,512,6,64]{1,3,2,0:T(8,128)(2,1)} %get-tuple-element.408, s32[]{:T(128)} %get-tuple-element.407, bf16[1024,6,64]{0,2,1:T(8,128)(2,1)S(1)} %copy-done.10, f32[6,512,1024]{2,1,0:T(8,128)S(1)} %get-tuple-element.378, f32[6,512]{1,0:T(8,128)S(1)} %fusion.213, ...), kind=kOutput, calls=%fused_computation.8.clone.1 | convolution fusion | flops 418578432 | bytes 14311936 | tf_op jit(solution)/shard_map/while/body/eval_jaxpr/hqk,khd->qhd/dot_general | solution.py:94
  51.5 5.0 %fusion.214 = bf16[2,512,6,64]{1,3,2,0:T(8,128)(2,1)} fusion(bf16[2,512,6,64]{1,3,2,0:T(8,128)(2,1)} %get-tuple-element.408, s32[]{:T(128)} %get-tuple-element.407, bf16[1024,6,64]{0,2,1:T(8,128)(2,1)S(1)} %copy-done.10, f32[6,512,1024]{2,1,0:T(8,128)S(1)} %get-tuple-element.378, f32[6,512]{1,0:T(8,128)S(1)} %fusion.213, ...), kind=kOutput, calls=%fused_computation.8.clone.1 | convolution fusion | flops 418578432 | bytes 14311936 | tf_op jit(solution)/shard_map/while/body/eval_jaxpr/hqk,khd->qhd/dot_general | solution.py:94
  61.6 12.1 %reduce-scatter.5.cloned.1.call-done = f32[512,768]{1,0:T(8,128)} async-done(((f32[1024,768]{1,0:T(8,128)}), f32[512,768]{1,0:T(8,128)}) %reduce-scatter.5.cloned.1.call-update) | async-done | bytes 1572880 | tf_op jit(solution)/shard_map/reduce_scatter | solution.py:190
  81.6 10.6 %all-gather.7.cloned.1.call-done = bf16[1024,768]{1,0:T(8,128)(2,1)} async-done(((bf16[512,768]{1,0:T(8,128)(2,1)}), bf16[1024,768]{1,0:T(8,128)(2,1)}) %all-gather.7.cloned.1.call-update) | async-done | bytes 1572880 | tf_op jit(solution)/shard_map/all_gather | solution.py:205
  99.0 17.3 %fusion.53 = bf16[1024,768]{1,0:T(8,128)(2,1)} fusion(bf16[1536,768]{1,0:T(8,128)(2,1)S(1)} %copy-done.52, f32[1024,1536]{1,0:T(8,128)S(1)} %fusion.147), kind=kOutput, calls=%fused_computation.78 | convolution fusion | flops 2518941696 | bytes 10223616 | tf_op jit(solution)/shard_map/dot_general | solution.py:211
  116.5 10.3 %reduce-scatter.7.cloned.1.call-done = bf16[512,768]{1,0:T(8,128)(2,1)} async-done(((bf16[1024,768]{1,0:T(8,128)(2,1)}), bf16[512,768]{1,0:T(8,128)(2,1)}) %reduce-scatter.7.cloned.1.call-update) | async-done | bytes 786448 | tf_op jit(solution)/shard_map/reduce_scatter | solution.py:210
  138.0 11.1 %all-gather.9.cloned.1.call-done = bf16[1024,768]{1,0:T(8,128)(2,1)} async-done(((bf16[512,768]{1,0:T(8,128)(2,1)}), bf16[1024,768]{1,0:T(8,128)(2,1)}) %all-gather.9.cloned.1.call-update) | async-done | bytes 1572880 | tf_op jit(solution)/shard_map/all_gather | solution.py:235
  149.1 10.5 %convolution_convert_fusion = bf16[1024,768]{1,0:T(8,128)(2,1)} fusion(bf16[768,1536]{1,0:T(8,128)(2,1)S(1)} %copy-done, f32[1024,1536]{1,0:T(8,128)} %copy-done.56, bf16[1024,768]{1,0:T(8,128)(2,1)} %all-gather.9.cloned.1.call-done, bf16[1536,768]{1,0:T(8,128)(2,1)} %param.32), kind=kOutput, calls=%fused_computation.79 | convolution fusion | flops 4848353280 | bytes 14155776 | tf_op jit(solution)/shard_map/dot_general | solution.py:23
  159.8 10.2 %reduce-scatter.9.cloned.1.call-done = bf16[512,768]{1,0:T(8,128)(2,1)} async-done(((bf16[1024,768]{1,0:T(8,128)(2,1)}), bf16[512,768]{1,0:T(8,128)(2,1)}) %reduce-scatter.9.cloned.1.call-update) | async-done | bytes 786448 | tf_op jit(solution)/shard_map/reduce_scatter | solution.py:238
  177.8 11.1 %all-gather.11.cloned.1.call-done = bf16[1024,768]{1,0:T(8,128)(2,1)} async-done(((bf16[512,768]{1,0:T(8,128)(2,1)}), bf16[1024,768]{1,0:T(8,128)(2,1)}) %all-gather.11.cloned.1.call-update) | async-done | bytes 1572880 | tf_op jit(solution)/shard_map/all_gather | solution.py:251
  192.9 98.8 %while.28 = (s32[]{:T(128)}, f32[1024,6,64]{0,2,1:T(8,128)S(1)}, f32[1024,6,64]{0,2,1:T(8,128)}, bf16[2,512,6,64]{1,3,2,0:T(8,128)(2,1)}, s32[2]{0:T(128)S(1)}, ...) while((s32[]{:T(128)}, f32[1024,6,64]{0,2,1:T(8,128)S(1)}, ...), condition=%wide.region_17.18_spmd.clone, body=%wide.region_15.17_spmd.clone.sunk | while | flops 2063332352 | bytes 179538384 | solution.py:135
  194.2 7.4 %fusion.224 = f32[6,512,1024]{2,1,0:T(8,128)} fusion(bf16[1024,6,64]{0,2,1:T(8,128)(2,1)S(1)} %get-tuple-element.475, bf16[1024,6,64]{0,2,1:T(8,128)(2,1)} %get-tuple-element.472, s32[]{:T(128)S(6)} %select_n.64), kind=kOutput, calls=%fused_computation.33.clone.1 | convolution fusion | flops 402653184 | bytes 13762564 | tf_op jit(solution)/shard_map/while/body/eval_jaxpr/qhd,khd->hqk/dot_general | solution.py:76
  204.0 11.6 %multiply_reduce_fusion.9 = (f32[6,512]{1,0:T(8,128)S(1)}, f32[6,512,1024]{2,1,0:T(8,128)}) fusion(f32[6,512,1024]{2,1,0:T(8,128)} %fusion.224, f32[6,512]{1,0:T(8,128)S(1)} %dynamic-slice_bitcast_fusion.2, pred[512,1024]{1,0:T(8,128)(4,1)S(1)} %broadcast_compare_fusion.5, bf16[1024,6,64]{0,2,1:T(8,128)(2,1)} %get-tuple-element.478, ...), kind=kOutput, calls=%fused_computation.17.clone.1 | convolution fusion | flops 418378752 | bytes 26894340 | tf_op jit(solution)/shard_map/while/body/eval_jaxpr/qhd,khd->hqk/dot_general | solution.py:118
  216.9 9.6 %multiply_convert_fusion.2 = bf16[6,512,1024]{2,1,0:T(8,128)(2,1)} fusion(f32[6,512,1024]{2,1,0:T(8,128)} %get-tuple-element.392, f32[6,512,1024]{2,1,0:T(8,128)S(1)} %bitcast.121, f32[6,512]{1,0:T(8,128)S(1)} %get-tuple-element.393, f32[6,512]{1,0:T(8,128)S(1)} %dynamic-slice_bitcast_fusion.2, pred[512,1024]{1,0:T(8,128)(4,1)S(1)} %broadcast_compare_fusion.5), kind=kLoop, calls=%fused_computation.16.clone.1 | loop fusion | flops 18874368 | bytes 32006144 | tf_op jit(solution)/shard_map/while/body/eval_jaxpr/convert_element_type | solution.py:123
  226.6 4.4 bitcast_add_fusion.4
  234.3 7.7 %bitcast_add_fusion.5 = f32[1024,6,64]{0,2,1:T(8,128)} fusion(f32[1024,6,64]{0,2,1:T(8,128)} %get-tuple-element.452, f32[6,512,1024]{2,1,0:T(8,128)} %fusion.224, f32[6,512]{1,0:T(8,128)S(1)} %dynamic-slice_bitcast_fusion.2, pred[512,1024]{1,0:T(8,128)(4,1)S(1)} %broadcast_compare_fusion.5, pred[]{:T(512)S(6)} %compare.3, ...), kind=kOutput, calls=%fused_computation.22.clone.1 | convolution fusion | flops 416022528 | bytes 16662533 | tf_op jit(solution)/shard_map/while/body/eval_jaxpr/hqk,qhd->khd/dot_general | solution.py:112
  243.3 7.4 %fusion.224 = f32[6,512,1024]{2,1,0:T(8,128)} fusion(bf16[1024,6,64]{0,2,1:T(8,128)(2,1)S(1)} %get-tuple-element.475, bf16[1024,6,64]{0,2,1:T(8,128)(2,1)} %get-tuple-element.472, s32[]{:T(128)S(6)} %select_n.64), kind=kOutput, calls=%fused_computation.33.clone.1 | convolution fusion | flops 402653184 | bytes 13762564 | tf_op jit(solution)/shard_map/while/body/eval_jaxpr/qhd,khd->hqk/dot_general | solution.py:76
  253.1 11.6 %multiply_reduce_fusion.9 = (f32[6,512]{1,0:T(8,128)S(1)}, f32[6,512,1024]{2,1,0:T(8,128)}) fusion(f32[6,512,1024]{2,1,0:T(8,128)} %fusion.224, f32[6,512]{1,0:T(8,128)S(1)} %dynamic-slice_bitcast_fusion.2, pred[512,1024]{1,0:T(8,128)(4,1)S(1)} %broadcast_compare_fusion.5, bf16[1024,6,64]{0,2,1:T(8,128)(2,1)} %get-tuple-element.478, ...), kind=kOutput, calls=%fused_computation.17.clone.1 | convolution fusion | flops 418378752 | bytes 26894340 | tf_op jit(solution)/shard_map/while/body/eval_jaxpr/qhd,khd->hqk/dot_general | solution.py:118
  266.0 9.6 %multiply_convert_fusion.2 = bf16[6,512,1024]{2,1,0:T(8,128)(2,1)} fusion(f32[6,512,1024]{2,1,0:T(8,128)} %get-tuple-element.392, f32[6,512,1024]{2,1,0:T(8,128)S(1)} %bitcast.121, f32[6,512]{1,0:T(8,128)S(1)} %get-tuple-element.393, f32[6,512]{1,0:T(8,128)S(1)} %dynamic-slice_bitcast_fusion.2, pred[512,1024]{1,0:T(8,128)(4,1)S(1)} %broadcast_compare_fusion.5), kind=kLoop, calls=%fused_computation.16.clone.1 | loop fusion | flops 18874368 | bytes 32006144 | tf_op jit(solution)/shard_map/while/body/eval_jaxpr/convert_element_type | solution.py:123
  283.4 8.1 %bitcast_add_fusion.5 = f32[1024,6,64]{0,2,1:T(8,128)} fusion(f32[1024,6,64]{0,2,1:T(8,128)} %get-tuple-element.452, f32[6,512,1024]{2,1,0:T(8,128)} %fusion.224, f32[6,512]{1,0:T(8,128)S(1)} %dynamic-slice_bitcast_fusion.2, pred[512,1024]{1,0:T(8,128)(4,1)S(1)} %broadcast_compare_fusion.5, pred[]{:T(512)S(6)} %compare.3, ...), kind=kOutput, calls=%fused_computation.22.clone.1 | convolution fusion | flops 416022528 | bytes 16662533 | tf_op jit(solution)/shard_map/while/body/eval_jaxpr/hqk,qhd->khd/dot_general | solution.py:112
  305.7 41.6 %all-reduce = (f32[64]{0:T(128)}, f32[768]{0:T(1024)}, f32[64]{0:T(128)}, f32[768]{0:T(1024)}, f32[768]{0:T(1024)}, /*index=5*/f32[768]{0:T(1024)}, f32[768]{0:T...) all-reduce(f32[64]{0:T(128)S(1)} %copy-done.51, ...), channel_id=1, replica_groups=mesh['dp'=16,'mp'=2] {'dp','mp'}, use_global_device_ids=true, to_apply=%region_21.22 | all-reduce | flops 4739 | bytes 37912 | tf_op jit(solution)/shard_map/psum | solution.py:270
  352.4 96.0 %all-reduce.4.cloned.1.call-done = (f32[768,64]{0,1:T(8,128)}, f32[64,768]{1,0:T(8,128)}, f32[768,64]{0,1:T(8,128)}, f32[64,768]{1,0:T(8,128)}) async-done(((f32[768,64]{0,1:T(8,128)}, f32[64,768]{1,0:T(8,128)}, f32[768,64]{0,1:T(8,128)}, f32[64,768]{1,0:T(8,128)}), (f32[768,64]{0,1:T(8,128)}, f32[64,768]{1,0:T(8,128)}, f32[768,64]{0,1:T(8,128)}, f32[64,768]{1,0:T(8,128)})) %all-reduce.4.cloned.1.call-update) | async-done | bytes 786448 | tf_op jit(solution)/shard_map/psum | solution.py:270
  (242 shorter events, 107.8 us)
Async XLA Ops:
  7.2 85.0 %copy-start = (bf16[768,1536]{1,0:T(8,128)(2,1)S(1)}, bf16[768,1536]{1,0:T(8,128)(2,1)}, u32[]{:S(2)}) copy-start(bf16[768,1536]{1,0:T(8,128)(2,1)} %param.31) | copy-start | bytes 7077892
  7.2 14.9 %all-gather.5.cloned.1.call-start = ((), (), s32[]{:S(2)}) async-start(), calls=%async_computation.4 | async-start | bytes 2359296 | tf_op jit(solution)/shard_map/all_gather | solution.py:176
  7.9 65.7 %reduce-scatter.5.cloned.1.call-start = ((), (), s32[]{:S(2)}) async-start(), calls=%async_computation.5 | async-start | bytes 4718592 | tf_op jit(solution)/shard_map/reduce_scatter | solution.py:190
  58.7 14.9 %copy-start.34 = (bf16[768,64]{0,1:T(8,128)(2,1)S(1)}, bf16[768,64]{0,1:T(8,128)(2,1)}, u32[]{:S(2)}) copy-start(bf16[768,64]{0,1:T(8,128)(2,1)} %param.33) | copy-start | bytes 294916
  61.4 14.0 %copy-start.36 = (bf16[64,768]{1,0:T(8,128)(2,1)S(1)}, bf16[64,768]{1,0:T(8,128)(2,1)}, u32[]{:S(2)}) copy-start(bf16[64,768]{1,0:T(8,128)(2,1)} %param.35) | copy-start | bytes 294916
  61.4 30.7 %all-gather.7.cloned.1.call-start = ((), (), s32[]{:S(2)}) async-start(), calls=%async_computation.6 | async-start | bytes 2359296 | tf_op jit(solution)/shard_map/all_gather | solution.py:205
  75.4 99.8 %copy-start.31 = (f32[512,64]{0,1:T(8,128)}, f32[512,64]{0,1:T(8,128)S(1)}, u32[]{:S(2)}) copy-start(f32[512,64]{0,1:T(8,128)S(1)} %convolution_add_fusion.3) | copy-start | bytes 393220
  81.0 45.7 %reduce-scatter.7.cloned.1.call-start = ((), (), s32[]{:S(2)}) async-start(), calls=%async_computation.7 | async-start | bytes 2359296 | tf_op jit(solution)/shard_map/reduce_scatter | solution.py:210
  99.0 17.4 %copy-start.55 = (bf16[64]{0:T(256)(128)(2,1)S(1)}, bf16[64]{0:T(256)(128)(2,1)}, u32[]{:S(2)}) copy-start(bf16[64]{0:T(256)(128)(2,1)} %param.38) | copy-start | bytes 388
  99.0 17.5 %copy-start.47 = (bf16[768]{0:T(1024)(128)(2,1)S(1)}, bf16[768]{0:T(1024)(128)(2,1)}, u32[]{:S(2)}) copy-start(bf16[768]{0:T(1024)(128)(2,1)} %param.40) | copy-start | bytes 4612
  99.0 17.5 %copy-start.48 = (bf16[768]{0:T(1024)(128)(2,1)S(1)}, bf16[768]{0:T(1024)(128)(2,1)}, u32[]{:S(2)}) copy-start(bf16[768]{0:T(1024)(128)(2,1)} %param.43) | copy-start | bytes 4612
  99.0 17.5 %copy-start.49 = (bf16[768]{0:T(1024)(128)(2,1)S(1)}, bf16[768]{0:T(1024)(128)(2,1)}, u32[]{:S(2)}) copy-start(bf16[768]{0:T(1024)(128)(2,1)} %param.44) | copy-start | bytes 4612
  99.0 27.8 %copy-start.33 = (bf16[768,64]{0,1:T(8,128)(2,1)S(1)}, bf16[768,64]{0,1:T(8,128)(2,1)}, u32[]{:S(2)}) copy-start(bf16[768,64]{0,1:T(8,128)(2,1)} %param.37) | copy-start | bytes 294916
  116.4 32.7 %all-gather.9.cloned.1.call-start = ((), (), s32[]{:S(2)}) async-start(), calls=%async_computation.8 | async-start | bytes 2359296 | tf_op jit(solution)/shard_map/all_gather | solution.py:235
  137.9 32.0 %reduce-scatter.9.cloned.1.call-start = ((), (), s32[]{:S(2)}) async-start(), calls=%async_computation.9 | async-start | bytes 2359296 | tf_op jit(solution)/shard_map/reduce_scatter | solution.py:238
  159.5 14.5 %copy-start.4 = (f32[512,768]{1,0:T(8,128)S(1)}, f32[512,768]{1,0:T(8,128)}, u32[]{:S(2)}) copy-start(f32[512,768]{1,0:T(8,128)} %copy-done.3) | copy-start | bytes 4718596
  159.5 29.3 %all-gather.11.cloned.1.call-start = ((), (), s32[]{:S(2)}) async-start(), calls=%async_computation.10 | async-start | bytes 2359296 | tf_op jit(solution)/shard_map/all_gather | solution.py:251
  175.3 13.6 %copy-start.19 = (bf16[384,768]{1,0:T(8,128)(2,1)S(1)}, bf16[384,768]{1,0:T(8,128)(2,1)}, u32[]{:S(2)}) copy-start(bf16[384,768]{1,0:T(8,128)(2,1)} %param.30) | copy-start | bytes 1769476
  176.2 15.7 %copy-start.27 = (bf16[512,64]{0,1:T(8,128)(2,1)}, bf16[512,64]{0,1:T(8,128)(2,1)S(1)}, u32[]{:S(2)}) copy-start(bf16[512,64]{0,1:T(8,128)(2,1)S(1)} %get-tuple-element.253) | copy-start | bytes 196612
  177.7 172.1 %reduce-scatter.11.cloned.1.call-start = ((), (), s32[]{:S(2)}) async-start(), calls=%async_computation.11 | async-start | bytes 2359296 | tf_op jit(solution)/shard_map/reduce_scatter | solution.py:263
  204.0 13.0 %slice-start.2 = ((s8[12582912]{0:T(1024)(128)(4,1)}), s8[4194304]{0:T(1024)(128)(4,1)S(1)}, s32[]{:S(2)}) async-start(s8[12582912]{0:T(1024)(128)(4,1)} %bitcast.120), calls=%async_computation.15 | async-start | bytes 8388608 | tf_op jit(solution)/shard_map/while
  253.0 13.0 %slice-start.2 = ((s8[12582912]{0:T(1024)(128)(4,1)}), s8[4194304]{0:T(1024)(128)(4,1)S(1)}, s32[]{:S(2)}) async-start(s8[12582912]{0:T(1024)(128)(4,1)} %bitcast.120), calls=%async_computation.15 | async-start | bytes 8388608 | tf_op jit(solution)/shard_map/while
  299.9 148.5 %all-reduce.4.cloned.1.call-start = ((), (), s32[]{:S(2)}) async-start(), calls=%async_computation.12 | async-start | bytes 1572864 | tf_op jit(solution)/shard_map/psum | solution.py:270
  304.4 150.4 %copy-start.1 = (bf16[768,1536]{1,0:T(8,128)(2,1)S(1)}, bf16[768,1536]{1,0:T(8,128)(2,1)}, u32[]{:S(2)}) copy-start(bf16[768,1536]{1,0:T(8,128)(2,1)} %param.31) | copy-start | bytes 7077892
  (53 other events, 195.6 us)
Sparse Core Ops, SparseCore 0:
  9.6 12.4 all-gather.4
  61.6 12.0 reduce-scatter.4
  81.2 10.9 all-gather.6
  116.5 10.2 reduce-scatter.6
  138.0 10.9 all-gather.8
  159.7 10.2 reduce-scatter.8
  177.8 10.9 all-gather.10
  300.0 10.2 reduce-scatter.10
  317.1 131.2 all-reduce.3
where the time goes:
time: 470 us; the launch traced here: 462 us
  waiting for transfers between devices  176 us (37%)
  matrix products  151 us (32%)
  other arithmetic  44.7 us (10%)
  blocking collectives  41.6 us (9%)
  local copies, waits for them, and re-layouts  25.2 us (5%)
  between operations  14.7 us (3%)
  loops' own time  6.91 us (1%)
    psum x1, waiting for transfers between devices, per_device(): lax.psum((mixer_grads[0], mixer_grads[1], mixer_grads[2], mixer_grads[3],...  96 us
    psum x1, blocking collectives, per_device(): lax.psum((mixer_grads[0], mixer_grads[1], mixer_grads[2], mixer_grads[3],...  41.6 us
    dot_general x2, matrix products, one_block(): jnp.einsum('qhd,khd->hqk', grad_rows, values, preferred_element_type=jnp....  23.3 us
    dot_general x9, matrix products, times_transpose(): lax.dot_general(left, right, (((1,), (1,)), ((), ())), preferred_element_...  22.3 us
    dot_general x4, matrix products, score_block(): jnp.einsum('qhd,khd->hqk', query_rows, keys, preferred_element_type=jnp.f...  21.5 us
    convert_element_type x2, other arithmetic, one_block(): score_grad = (shares * (share_grad - jnp.sum(shares * share_grad, -1, kee...  19.2 us
    dot_general x1, matrix products, per_device(): jnp.dot(inner_low, outer_weight, preferred_element_type=jnp.float32)  17.3 us
    dot_general x2, matrix products, one_block(): jnp.einsum('hqk,qhd->khd', shares.astype(jnp.bfloat16), grad_rows, prefer...  15.8 us
  transfers between devices with their start and end apart: 9, of which 8 were waited for; matrix products, arithmetic and copies ran while one was open for 2% of the time, Pallas kernels for 0%

commit v1 on v0

--- a/solution.py
+++ b/solution.py
@@ -268,21 +268,24 @@
     ).astype(jnp.float32)
     input_grad = (first_grad + input_back).astype(jnp.bfloat16)
     summed = lax.psum(
-        (
-            mixer_grads[0],
-            mixer_grads[1],
-            mixer_grads[2],
-            mixer_grads[3],
-            dense_grads[0],
-            dense_grads[1],
-            dense_grads[2],
-            dense_grads[3],
-            first_gain_grad,
-            first_shift_grad,
-            second_gain_grad,
-            second_shift_grad,
+        lax.psum(
+            (
+                mixer_grads[0],
+                mixer_grads[1],
+                mixer_grads[2],
+                mixer_grads[3],
+                dense_grads[0],
+                dense_grads[1],
+                dense_grads[2],
+                dense_grads[3],
+                first_gain_grad,
+                first_shift_grad,
+                second_gain_grad,
+                second_shift_grad,
+            ),
+            "mp",
         ),
-        ("dp", "mp"),
+        "dp",
     )
     ratios = jnp.sqrt(jnp.stack([mixer_square, dense_square]) / input_square)
     return (

time: 470 us -> 452 us (0.962)
  waiting for transfers between devices: 176 us -> 78 us
  blocking collectives: 41.6 us -> 121 us
    psum x0 -> x2, blocking collectives: none -> 117 us  [the longest x1 76 us: per_device(): lax.psum(lax.psum((mixer_grads[0], mixer_grads[1], mixer_grads[2], mixer_...]
    psum x1, waiting for transfers between devices: 96 us -> 0.02 us  [per_device(): lax.psum((mixer_grads[0], mixer_grads[1], mixer_grads[2], mixer_grads[3],...]
    psum x1, blocking collectives: 41.6 us -> 3.44 us  [per_device(): lax.psum((mixer_grads[0], mixer_grads[1], mixer_grads[2], mixer_grads[3],...]
    all_gather x1, waiting for transfers between devices: 11.1 us -> 5.28 us  [per_device(): lax.all_gather(attended_grad, 'mp', axis=0, tiled=True)]
    unnamed x110 -> x102, local copies, waits for them, and re-layouts: 11.3 us -> 10.8 us
  transfers between devices with their start and end apart: 9 -> 10, of which waited for: 8 -> 8; matrix products, arithmetic and copies ran while one was open for 2% -> 25% of each run, Pallas kernels for 0% -> 0%
where the time goes in v1:
time: 452 us; the launch traced here: 443 us
  matrix products  151 us (33%)
  blocking collectives  121 us (27%)
  waiting for transfers between devices  78 us (17%)
  other arithmetic  44.9 us (10%)
  local copies, waits for them, and re-layouts  25 us (6%)
  between operations  15.2 us (3%)
  loops' own time  6.82 us (2%)
    psum x1, blocking collectives, per_device(): lax.psum(lax.psum((mixer_grads[0], mixer_grads[1], mixer_grads[2], mixer_...  76 us
    psum x1, blocking collectives, per_device(): lax.psum((mixer_square, dense_square, input_square), ('dp', 'mp'))  41.1 us
    dot_general x2, matrix products, one_block(): jnp.einsum('qhd,khd->hqk', grad_rows, values, preferred_element_type=jnp....  23.3 us
    dot_general x9, matrix products, times_transpose(): lax.dot_general(left, right, (((1,), (1,)), ((), ())), preferred_element_...  22.5 us
    dot_general x4, matrix products, score_block(): jnp.einsum('qhd,khd->hqk', query_rows, keys, preferred_element_type=jnp.f...  21.5 us
    convert_element_type x2, other arithmetic, one_block(): score_grad = (shares * (share_grad - jnp.sum(shares * share_grad, -1, kee...  19.3 us
    dot_general x1, matrix products, per_device(): jnp.dot(inner_low, outer_weight, preferred_element_type=jnp.float32)  17.3 us
    dot_general x2, matrix products, one_block(): jnp.einsum('hqk,qhd->khd', shares.astype(jnp.bfloat16), grad_rows, prefer...  15.7 us
  transfers between devices with their start and end apart: 10, of which 8 were waited for; matrix products, arithmetic and copies ran while one was open for 25% of the time, Pallas kernels for 0%

profile of v1, /device:TPU:0, one launch (start us, length us, event | category | flops | bytes accessed | tf_op | source)
XLA Modules:
  0.0 442.7 jit_solution(10218108139405424064)
XLA Ops:
  8.0 14.1 %all-gather.5.cloned.1.call-done = bf16[1024,768]{1,0:T(8,128)(2,1)} async-done(((bf16[512,768]{1,0:T(8,128)(2,1)}), bf16[1024,768]{1,0:T(8,128)(2,1)}) %all-gather.5.cloned.1.call-update) | async-done | bytes 1572880 | tf_op jit(solution)/shard_map/all_gather | solution.py:176
  29.1 27.5 %while.27 = (s32[]{:T(128)}, bf16[2,512,6,64]{1,3,2,0:T(8,128)(2,1)}, f32[2,6,512]{2,1,0:T(8,128)S(1)}, s32[2]{0:T(128)S(1)}, s32[1024]{0:T(1024)S(1)}, /*index=...) while((s32[]{:T(128)}, ...), condition=%wide.region_3.4_spmd, body=%wide.region_0.3_spmd.sunk | while | flops 843772928 | bytes 45472476 | solution.py:97
  37.8 5.0 %fusion.214 = bf16[2,512,6,64]{1,3,2,0:T(8,128)(2,1)} fusion(bf16[2,512,6,64]{1,3,2,0:T(8,128)(2,1)} %get-tuple-element.420, s32[]{:T(128)} %get-tuple-element.419, bf16[1024,6,64]{0,2,1:T(8,128)(2,1)S(1)} %copy-done.9, f32[6,512,1024]{2,1,0:T(8,128)S(1)} %get-tuple-element.390, f32[6,512]{1,0:T(8,128)S(1)} %fusion.213, ...), kind=kOutput, calls=%fused_computation.8.clone.1 | convolution fusion | flops 418578432 | bytes 14311936 | tf_op jit(solution)/shard_map/while/body/eval_jaxpr/hqk,khd->qhd/dot_general | solution.py:94
  51.6 5.0 %fusion.214 = bf16[2,512,6,64]{1,3,2,0:T(8,128)(2,1)} fusion(bf16[2,512,6,64]{1,3,2,0:T(8,128)(2,1)} %get-tuple-element.420, s32[]{:T(128)} %get-tuple-element.419, bf16[1024,6,64]{0,2,1:T(8,128)(2,1)S(1)} %copy-done.9, f32[6,512,1024]{2,1,0:T(8,128)S(1)} %get-tuple-element.390, f32[6,512]{1,0:T(8,128)S(1)} %fusion.213, ...), kind=kOutput, calls=%fused_computation.8.clone.1 | convolution fusion | flops 418578432 | bytes 14311936 | tf_op jit(solution)/shard_map/while/body/eval_jaxpr/hqk,khd->qhd/dot_general | solution.py:94
  61.6 12.1 %reduce-scatter.5.cloned.1.call-done = f32[512,768]{1,0:T(8,128)} async-done(((f32[1024,768]{1,0:T(8,128)}), f32[512,768]{1,0:T(8,128)}) %reduce-scatter.5.cloned.1.call-update) | async-done | bytes 1572880 | tf_op jit(solution)/shard_map/reduce_scatter | solution.py:190
  81.2 10.9 %all-gather.7.cloned.1.call-done = bf16[1024,768]{1,0:T(8,128)(2,1)} async-done(((bf16[512,768]{1,0:T(8,128)(2,1)}), bf16[1024,768]{1,0:T(8,128)(2,1)}) %all-gather.7.cloned.1.call-update) | async-done | bytes 1572880 | tf_op jit(solution)/shard_map/all_gather | solution.py:205
  98.9 17.3 %fusion.53 = bf16[1024,768]{1,0:T(8,128)(2,1)} fusion(bf16[1536,768]{1,0:T(8,128)(2,1)S(1)} %copy-done.48, f32[1024,1536]{1,0:T(8,128)S(1)} %fusion.147), kind=kOutput, calls=%fused_computation.78 | convolution fusion | flops 2518941696 | bytes 10223616 | tf_op jit(solution)/shard_map/dot_general | solution.py:211
  116.4 10.3 %reduce-scatter.7.cloned.1.call-done = bf16[512,768]{1,0:T(8,128)(2,1)} async-done(((bf16[1024,768]{1,0:T(8,128)(2,1)}), bf16[512,768]{1,0:T(8,128)(2,1)}) %reduce-scatter.7.cloned.1.call-update) | async-done | bytes 786448 | tf_op jit(solution)/shard_map/reduce_scatter | solution.py:210
  137.4 11.1 %all-gather.9.cloned.1.call-done = bf16[1024,768]{1,0:T(8,128)(2,1)} async-done(((bf16[512,768]{1,0:T(8,128)(2,1)}), bf16[1024,768]{1,0:T(8,128)(2,1)}) %all-gather.9.cloned.1.call-update) | async-done | bytes 1572880 | tf_op jit(solution)/shard_map/all_gather | solution.py:235
  148.5 10.5 %convolution_convert_fusion = bf16[1024,768]{1,0:T(8,128)(2,1)} fusion(bf16[768,1536]{1,0:T(8,128)(2,1)S(1)} %copy-done, f32[1024,1536]{1,0:T(8,128)} %copy-done.52, bf16[1024,768]{1,0:T(8,128)(2,1)} %all-gather.9.cloned.1.call-done, bf16[1536,768]{1,0:T(8,128)(2,1)} %param.32), kind=kOutput, calls=%fused_computation.79 | convolution fusion | flops 4848353280 | bytes 14155776 | tf_op jit(solution)/shard_map/dot_general | solution.py:23
  159.3 10.1 %reduce-scatter.9.cloned.1.call-done = bf16[512,768]{1,0:T(8,128)(2,1)} async-done(((bf16[1024,768]{1,0:T(8,128)(2,1)}), bf16[512,768]{1,0:T(8,128)(2,1)}) %reduce-scatter.9.cloned.1.call-update) | async-done | bytes 786448 | tf_op jit(solution)/shard_map/reduce_scatter | solution.py:238
  183.1 5.3 %all-gather.11.cloned.1.call-done = bf16[1024,768]{1,0:T(8,128)(2,1)} async-done(((bf16[512,768]{1,0:T(8,128)(2,1)}), bf16[1024,768]{1,0:T(8,128)(2,1)}) %all-gather.11.cloned.1.call-update) | async-done | bytes 1572880 | tf_op jit(solution)/shard_map/all_gather | solution.py:251
  192.4 99.0 %while.28 = (s32[]{:T(128)}, f32[1024,6,64]{0,2,1:T(8,128)S(1)}, f32[1024,6,64]{0,2,1:T(8,128)}, bf16[2,512,6,64]{1,3,2,0:T(8,128)(2,1)}, s32[2]{0:T(128)S(1)}, ...) while((s32[]{:T(128)}, f32[1024,6,64]{0,2,1:T(8,128)S(1)}, ...), condition=%wide.region_17.18_spmd.clone, body=%wide.region_15.17_spmd.clone.sunk | while | flops 2063332352 | bytes 179538384 | solution.py:135
  193.7 7.4 %fusion.224 = f32[6,512,1024]{2,1,0:T(8,128)} fusion(bf16[1024,6,64]{0,2,1:T(8,128)(2,1)S(1)} %get-tuple-element.487, bf16[1024,6,64]{0,2,1:T(8,128)(2,1)} %get-tuple-element.484, s32[]{:T(128)S(6)} %select_n.64), kind=kOutput, calls=%fused_computation.33.clone.1 | convolution fusion | flops 402653184 | bytes 13762564 | tf_op jit(solution)/shard_map/while/body/eval_jaxpr/qhd,khd->hqk/dot_general | solution.py:76
  203.5 11.7 %multiply_reduce_fusion.9 = (f32[6,512]{1,0:T(8,128)S(1)}, f32[6,512,1024]{2,1,0:T(8,128)}) fusion(f32[6,512,1024]{2,1,0:T(8,128)} %fusion.224, f32[6,512]{1,0:T(8,128)S(1)} %dynamic-slice_bitcast_fusion.2, pred[512,1024]{1,0:T(8,128)(4,1)S(1)} %broadcast_compare_fusion.5, bf16[1024,6,64]{0,2,1:T(8,128)(2,1)} %get-tuple-element.490, ...), kind=kOutput, calls=%fused_computation.17.clone.1 | convolution fusion | flops 418378752 | bytes 26894340 | tf_op jit(solution)/shard_map/while/body/eval_jaxpr/qhd,khd->hqk/dot_general | solution.py:118
  216.7 9.6 %multiply_convert_fusion.2 = bf16[6,512,1024]{2,1,0:T(8,128)(2,1)} fusion(f32[6,512,1024]{2,1,0:T(8,128)} %get-tuple-element.404, f32[6,512,1024]{2,1,0:T(8,128)S(1)} %bitcast.121, f32[6,512]{1,0:T(8,128)S(1)} %get-tuple-element.405, f32[6,512]{1,0:T(8,128)S(1)} %dynamic-slice_bitcast_fusion.2, pred[512,1024]{1,0:T(8,128)(4,1)S(1)} %broadcast_compare_fusion.5), kind=kLoop, calls=%fused_computation.16.clone.1 | loop fusion | flops 18874368 | bytes 32006144 | tf_op jit(solution)/shard_map/while/body/eval_jaxpr/convert_element_type | solution.py:123
  234.1 7.6 %bitcast_add_fusion.5 = f32[1024,6,64]{0,2,1:T(8,128)} fusion(f32[1024,6,64]{0,2,1:T(8,128)} %get-tuple-element.464, f32[6,512,1024]{2,1,0:T(8,128)} %fusion.224, f32[6,512]{1,0:T(8,128)S(1)} %dynamic-slice_bitcast_fusion.2, pred[512,1024]{1,0:T(8,128)(4,1)S(1)} %broadcast_compare_fusion.5, pred[]{:T(512)S(6)} %compare.3, ...), kind=kOutput, calls=%fused_computation.22.clone.1 | convolution fusion | flops 416022528 | bytes 16662533 | tf_op jit(solution)/shard_map/while/body/eval_jaxpr/hqk,qhd->khd/dot_general | solution.py:112
  243.0 7.4 %fusion.224 = f32[6,512,1024]{2,1,0:T(8,128)} fusion(bf16[1024,6,64]{0,2,1:T(8,128)(2,1)S(1)} %get-tuple-element.487, bf16[1024,6,64]{0,2,1:T(8,128)(2,1)} %get-tuple-element.484, s32[]{:T(128)S(6)} %select_n.64), kind=kOutput, calls=%fused_computation.33.clone.1 | convolution fusion | flops 402653184 | bytes 13762564 | tf_op jit(solution)/shard_map/while/body/eval_jaxpr/qhd,khd->hqk/dot_general | solution.py:76
  252.8 11.6 %multiply_reduce_fusion.9 = (f32[6,512]{1,0:T(8,128)S(1)}, f32[6,512,1024]{2,1,0:T(8,128)}) fusion(f32[6,512,1024]{2,1,0:T(8,128)} %fusion.224, f32[6,512]{1,0:T(8,128)S(1)} %dynamic-slice_bitcast_fusion.2, pred[512,1024]{1,0:T(8,128)(4,1)S(1)} %broadcast_compare_fusion.5, bf16[1024,6,64]{0,2,1:T(8,128)(2,1)} %get-tuple-element.490, ...), kind=kOutput, calls=%fused_computation.17.clone.1 | convolution fusion | flops 418378752 | bytes 26894340 | tf_op jit(solution)/shard_map/while/body/eval_jaxpr/qhd,khd->hqk/dot_general | solution.py:118
  265.7 9.6 %multiply_convert_fusion.2 = bf16[6,512,1024]{2,1,0:T(8,128)(2,1)} fusion(f32[6,512,1024]{2,1,0:T(8,128)} %get-tuple-element.404, f32[6,512,1024]{2,1,0:T(8,128)S(1)} %bitcast.121, f32[6,512]{1,0:T(8,128)S(1)} %get-tuple-element.405, f32[6,512]{1,0:T(8,128)S(1)} %dynamic-slice_bitcast_fusion.2, pred[512,1024]{1,0:T(8,128)(4,1)S(1)} %broadcast_compare_fusion.5), kind=kLoop, calls=%fused_computation.16.clone.1 | loop fusion | flops 18874368 | bytes 32006144 | tf_op jit(solution)/shard_map/while/body/eval_jaxpr/convert_element_type | solution.py:123
  275.4 4.4 bitcast_add_fusion.4
  283.2 8.1 %bitcast_add_fusion.5 = f32[1024,6,64]{0,2,1:T(8,128)} fusion(f32[1024,6,64]{0,2,1:T(8,128)} %get-tuple-element.464, f32[6,512,1024]{2,1,0:T(8,128)} %fusion.224, f32[6,512]{1,0:T(8,128)S(1)} %dynamic-slice_bitcast_fusion.2, pred[512,1024]{1,0:T(8,128)(4,1)S(1)} %broadcast_compare_fusion.5, pred[]{:T(512)S(6)} %compare.3, ...), kind=kOutput, calls=%fused_computation.22.clone.1 | convolution fusion | flops 416022528 | bytes 16662533 | tf_op jit(solution)/shard_map/while/body/eval_jaxpr/hqk,qhd->khd/dot_general | solution.py:112
  300.4 41.1 %all-reduce = (f32[1]{0:T(128)}, f32[1]{0:T(128)}, f32[]{:T(128)}) all-reduce(f32[1]{0:T(128)} %bitcast.13, f32[1]{0:T(128)} %bitcast.12, f32[]{:T(128)} %get-tuple-element.263), channel_id=1, replica_groups=mesh['dp'=16,'mp'=2] {'dp','mp'}, use_global_device_ids=true, to_apply=%region_54.55 | all-reduce | flops 3 | bytes 24 | tf_op jit(solution)/shard_map/psum | solution.py:225
  347.6 76.0 %all-reduce.1 = (f32[64]{0:T(128)}, f32[768]{0:T(1024)}, f32[64]{0:T(128)}, f32[768]{0:T(1024)}, f32[768]{0:T(1024)}, /*index=5*/f32[768]{0:T(1024)}, f32[768]{0:T(1024)}, f32[768]{0:T(1024)}) all-reduce(f32[64]{0:T(128)S(1)} %get-tuple-element.237, f32[768]{0:T(1024)S(1)} %get-tuple-element.238, ...), channel_id=1, replica_groups=mesh['dp'=16,'mp'=2] {'dp'}, use_global_device_ids=true, to_apply=%region_23.24 | all-reduce | flops 4736 | bytes 37888 | tf_op jit(solution)/shard_map/psum | solution.py:270
  (239 shorter events, 114.5 us)
Async XLA Ops:
  7.2 84.9 %copy-start = (bf16[768,1536]{1,0:T(8,128)(2,1)S(1)}, bf16[768,1536]{1,0:T(8,128)(2,1)}, u32[]{:S(2)}) copy-start(bf16[768,1536]{1,0:T(8,128)(2,1)} %param.31) | copy-start | bytes 7077892
  7.2 14.9 %all-gather.5.cloned.1.call-start = ((), (), s32[]{:S(2)}) async-start(), calls=%async_computation.4 | async-start | bytes 2359296 | tf_op jit(solution)/shard_map/all_gather | solution.py:176
  7.9 65.8 %reduce-scatter.5.cloned.1.call-start = ((), (), s32[]{:S(2)}) async-start(), calls=%async_computation.5 | async-start | bytes 4718592 | tf_op jit(solution)/shard_map/reduce_scatter | solution.py:190
  61.5 30.6 %all-gather.7.cloned.1.call-start = ((), (), s32[]{:S(2)}) async-start(), calls=%async_computation.6 | async-start | bytes 2359296 | tf_op jit(solution)/shard_map/all_gather | solution.py:205
  81.0 45.7 %reduce-scatter.7.cloned.1.call-start = ((), (), s32[]{:S(2)}) async-start(), calls=%async_computation.7 | async-start | bytes 2359296 | tf_op jit(solution)/shard_map/reduce_scatter | solution.py:210
  98.9 17.5 %copy-start.43 = (bf16[768]{0:T(1024)(128)(2,1)S(1)}, bf16[768]{0:T(1024)(128)(2,1)}, u32[]{:S(2)}) copy-start(bf16[768]{0:T(1024)(128)(2,1)} %param.40) | copy-start | bytes 4612
  98.9 17.5 %copy-start.44 = (bf16[768]{0:T(1024)(128)(2,1)S(1)}, bf16[768]{0:T(1024)(128)(2,1)}, u32[]{:S(2)}) copy-start(bf16[768]{0:T(1024)(128)(2,1)} %param.43) | copy-start | bytes 4612
  98.9 17.5 %copy-start.45 = (bf16[768]{0:T(1024)(128)(2,1)S(1)}, bf16[768]{0:T(1024)(128)(2,1)}, u32[]{:S(2)}) copy-start(bf16[768]{0:T(1024)(128)(2,1)} %param.44) | copy-start | bytes 4612
  98.9 27.8 %copy-start.25 = (bf16[768,64]{0,1:T(8,128)(2,1)S(1)}, bf16[768,64]{0,1:T(8,128)(2,1)}, u32[]{:S(2)}) copy-start(bf16[768,64]{0,1:T(8,128)(2,1)} %param.37) | copy-start | bytes 294916
  116.3 32.2 %all-gather.9.cloned.1.call-start = ((), (), s32[]{:S(2)}) async-start(), calls=%async_computation.8 | async-start | bytes 2359296 | tf_op jit(solution)/shard_map/all_gather | solution.py:235
  137.4 32.0 %reduce-scatter.9.cloned.1.call-start = ((), (), s32[]{:S(2)}) async-start(), calls=%async_computation.9 | async-start | bytes 2359296 | tf_op jit(solution)/shard_map/reduce_scatter | solution.py:238
  159.0 29.3 %all-gather.11.cloned.1.call-start = ((), (), s32[]{:S(2)}) async-start(), calls=%async_computation.10 | async-start | bytes 2359296 | tf_op jit(solution)/shard_map/all_gather | solution.py:251
  177.2 122.7 %all-reduce.10.cloned.1.call-start = ((), (), s32[]{:S(2)}) async-start(), calls=%async_computation.13 | async-start | bytes 1572864 | tf_op jit(solution)/shard_map/psum | solution.py:271
  183.0 240.6 %reduce-scatter.11.cloned.1.call-start = ((), (), s32[]{:S(2)}) async-start(), calls=%async_computation.11 | async-start | bytes 2359296 | tf_op jit(solution)/shard_map/reduce_scatter | solution.py:263
  297.4 46.7 %copy-start.34 = (f32[768]{0:T(1024)S(1)}, f32[768]{0:T(1024)}, u32[]{:S(2)}) copy-start(f32[768]{0:T(1024)} %get-tuple-element.174) | copy-start | bytes 9220
  297.4 46.7 %copy-start.35 = (f32[768]{0:T(1024)S(1)}, f32[768]{0:T(1024)}, u32[]{:S(2)}) copy-start(f32[768]{0:T(1024)} %get-tuple-element.179) | copy-start | bytes 9220
  297.4 46.7 %copy-start.36 = (f32[768]{0:T(1024)S(1)}, f32[768]{0:T(1024)}, u32[]{:S(2)}) copy-start(f32[768]{0:T(1024)} %get-tuple-element.171) | copy-start | bytes 9220
  297.4 46.7 %copy-start.37 = (f32[768]{0:T(1024)S(1)}, f32[768]{0:T(1024)}, u32[]{:S(2)}) copy-start(f32[768]{0:T(1024)} %get-tuple-element.176) | copy-start | bytes 9220
  297.5 46.7 %copy-start.38 = (f32[768]{0:T(1024)S(1)}, f32[768]{0:T(1024)}, u32[]{:S(2)}) copy-start(f32[768]{0:T(1024)} %get-tuple-element.177) | copy-start | bytes 9220
  297.5 46.7 %copy-start.39 = (f32[768]{0:T(1024)S(1)}, f32[768]{0:T(1024)}, u32[]{:S(2)}) copy-start(f32[768]{0:T(1024)} %get-tuple-element.249) | copy-start | bytes 9220
  297.5 46.7 %copy-start.46 = (f32[64]{0:T(128)S(1)}, f32[64]{0:T(128)}, u32[]{:S(2)}) copy-start(f32[64]{0:T(128)} %get-tuple-element.266) | copy-start | bytes 772
  297.5 46.7 %copy-start.47 = (f32[64]{0:T(128)S(1)}, f32[64]{0:T(128)}, u32[]{:S(2)}) copy-start(f32[64]{0:T(128)} %get-tuple-element.264) | copy-start | bytes 772
  299.8 135.6 %copy-start.1 = (bf16[768,1536]{1,0:T(8,128)(2,1)S(1)}, bf16[768,1536]{1,0:T(8,128)(2,1)}, u32[]{:S(2)}) copy-start(bf16[768,1536]{1,0:T(8,128)(2,1)} %param.31) | copy-start | bytes 7077892
  299.9 129.1 %all-reduce.8.cloned.1.call-start = ((), (), s32[]{:S(2)}) async-start(), calls=%async_computation.12 | async-start | bytes 1572864 | tf_op jit(solution)/shard_map/psum | solution.py:270
  (50 other events, 265.7 us)
Sparse Core Ops, SparseCore 0:
  9.6 12.4 all-gather.4
  61.6 12.0 reduce-scatter.4
  81.1 10.9 all-gather.6
  116.4 10.2 reduce-scatter.6
  137.5 10.9 all-gather.8
  159.1 10.2 reduce-scatter.8
  177.3 10.9 all-gather.10
  192.2 20.4 all-reduce.9
  300.0 10.2 reduce-scatter.10
  316.5 112.4 all-reduce.7
